TPU v7x, 128 devices: a whole 4x4x4 slice. The times are simulated.
128 devices in a mesh: rep: 4 (over x), shard: 32 (over z, y, core).
Axes of the slice: x: 4, y: 4, z: 4, core: 2. Of those that a mesh axis runs over, the one named last changes fastest.
Arguments:
- attention_grad: bfloat16 [4, 8, 768, 768], P('rep', None, 'shard'), may hold values from -45 to 45
- dense_grad: bfloat16 [4, 2, 3072, 768], P('rep', None, 'shard'), may hold values from -45 to 45
- embedding_grad: bfloat16 [4, 8192, 768], P('rep', 'shard'), may hold values from -45 to 45
- attention_error: float32 [4, 8, 768, 768], P('rep', None, 'shard'), may hold values from -4 to 4
- dense_error: float32 [4, 2, 3072, 768], P('rep', None, 'shard'), may hold values from -4 to 4
- embedding_error: float32 [4, 8192, 768], P('rep', 'shard'), may hold values from -4 to 4
- attention_weight: float32 [8, 768, 768], P(None, 'shard'), may hold values from -0.21875 to 0.21875
- dense_weight: float32 [2, 3072, 768], P(None, 'shard'), may hold values from -0.21875 to 0.21875
- embedding_weight: float32 [8192, 768], P('shard'), may hold values from -0.21875 to 0.21875
- attention_momentum: float32 [8, 768, 768], P(None, 'shard'), may hold values from -1.5 to 1.5
- dense_momentum: float32 [2, 3072, 768], P(None, 'shard'), may hold values from -1.5 to 1.5
- embedding_momentum: float32 [8192, 768], P('shard'), may hold values from -1.5 to 1.5
- warm_start: float32 [11, 32, 768], replicated, may hold values from -0.21875 to 0.21875
- norm_scale: float32 [3, 768], P(None, 'shard'), may hold values from 0.5 to 1.5
- norm_momentum: float32 [3, 768], P(None, 'shard'), may hold values from -1.5 to 1.5
- norm_grad: float32 [4, 3, 768], P('rep', None, 'shard'), may hold values from -6 to 6
Outputs:
- attention_updated: float32 [8, 768, 768], P(None, 'shard')
- dense_updated: float32 [2, 3072, 768], P(None, 'shard')
- embedding_updated: float32 [8192, 768], P('shard')
- attention_copy: bfloat16 [8, 768, 768], P(None, 'shard')
- dense_copy: bfloat16 [2, 3072, 768], P(None, 'shard')
- embedding_copy: bfloat16 [8192, 768], P('shard')
- attention_residue: float32 [4, 8, 768, 768], P('rep', None, 'shard')
- dense_residue: float32 [4, 2, 3072, 768], P('rep', None, 'shard')
- embedding_residue: float32 [4, 8192, 768], P('rep', 'shard')
- attention_velocity: float32 [8, 768, 768], P(None, 'shard')
- dense_velocity: float32 [2, 3072, 768], P(None, 'shard')
- embedding_velocity: float32 [8192, 768], P('shard')
- next_start: float32 [11, 32, 768], replicated
- norm_updated: float32 [3, 768], P(None, 'shard')
- norm_velocity: float32 [3, 768], P(None, 'shard')
All inputs are finite; a program needn't handle non-finite values.
Results may differ from a plain program's by a relative error of at most 0.001.
Values sent between devices are 32-bit elements; how exact they have to be, the bound alone decides.
A program may use at most 64 MiB of HBM per device.

v0:
```python
import jax
import jax.numpy as jnp
from jax import lax
from jax.sharding import PartitionSpec as P


def invert(grams):
    factor = jnp.linalg.cholesky(grams)
    identity = jnp.broadcast_to(jnp.eye(grams.shape[-1], dtype=grams.dtype), grams.shape)
    return lax.linalg.triangular_solve(factor, identity, left_side=True, lower=True)


def finish(merged, approx, weight, momentum):
    velocity = 0.9 * momentum + approx
    updated = weight - 0.05 * velocity
    return (updated, updated.astype(jnp.bfloat16), (merged - approx)[None], velocity)


def body(
    attention_grad,
    dense_grad,
    embedding_grad,
    attention_error,
    dense_error,
    embedding_error,
    attention_weight,
    dense_weight,
    embedding_weight,
    attention_momentum,
    dense_momentum,
    embedding_momentum,
    warm_start,
    norm_scale,
    norm_momentum,
    norm_grad,
):
    highest = lax.Precision.HIGHEST
    replicas = lax.axis_size("rep")
    norm_total = lax.psum(norm_grad[0], "rep")
    merged_attention = attention_grad[0].astype(jnp.float32) + attention_error[0]
    merged_dense = dense_grad[0].astype(jnp.float32) + dense_error[0]
    merged_embedding = embedding_grad[0].astype(jnp.float32) + embedding_error[0]
    proj_attention = jnp.einsum("mkc,mrc->mkr", warm_start[:8], merged_attention, precision=highest)
    proj_dense = jnp.einsum("mkc,mrc->mkr", warm_start[8:10], merged_dense, precision=highest)
    proj_embedding = jnp.einsum("kc,rc->kr", warm_start[10], merged_embedding, precision=highest)
    proj_attention, proj_dense, proj_embedding = lax.psum(
        (proj_attention, proj_dense, proj_embedding), "rep"
    )
    proj_attention = proj_attention / replicas
    proj_dense = proj_dense / replicas
    proj_embedding = proj_embedding / replicas
    local_grams = jnp.concatenate(
        [
            jnp.einsum("mkr,mjr->mkj", proj_attention, proj_attention, precision=highest),
            jnp.einsum("mkr,mjr->mkj", proj_dense, proj_dense, precision=highest),
            jnp.einsum("kr,jr->kj", proj_embedding, proj_embedding, precision=highest)[None],
        ],
        0,
    )
    grams = lax.psum(local_grams, "shard")
    inverse = invert(grams)
    ortho_attention = jnp.einsum("mjk,mkr->mjr", inverse[:8], proj_attention, precision=highest)
    ortho_dense = jnp.einsum("mjk,mkr->mjr", inverse[8:10], proj_dense, precision=highest)
    ortho_embedding = jnp.einsum("jk,kr->jr", inverse[10], proj_embedding, precision=highest)
    partial_right = jnp.concatenate(
        [
            jnp.einsum("mkr,mrc->mkc", ortho_attention, merged_attention, precision=highest),
            jnp.einsum("mkr,mrc->mkc", ortho_dense, merged_dense, precision=highest),
            jnp.einsum("kr,rc->kc", ortho_embedding, merged_embedding, precision=highest)[None],
        ],
        0,
    )
    next_start = lax.psum(partial_right, ("rep", "shard")) / replicas
    approx_attention = jnp.einsum(
        "mkr,mkc->mrc", ortho_attention, next_start[:8], precision=highest
    )
    approx_dense = jnp.einsum("mkr,mkc->mrc", ortho_dense, next_start[8:10], precision=highest)
    approx_embedding = jnp.einsum("kr,kc->rc", ortho_embedding, next_start[10], precision=highest)
    a_upd, a_copy, a_res, a_vel = finish(
        merged_attention, approx_attention, attention_weight, attention_momentum
    )
    d_upd, d_copy, d_res, d_vel = finish(merged_dense, approx_dense, dense_weight, dense_momentum)
    e_upd, e_copy, e_res, e_vel = finish(
        merged_embedding, approx_embedding, embedding_weight, embedding_momentum
    )
    norm_velocity = 0.9 * norm_momentum + norm_total / replicas
    norm_updated = norm_scale - 0.05 * norm_velocity
    return (
        a_upd,
        d_upd,
        e_upd,
        a_copy,
        d_copy,
        e_copy,
        a_res,
        d_res,
        e_res,
        a_vel,
        d_vel,
        e_vel,
        next_start,
        norm_updated,
        norm_velocity,
    )


def solution(mesh):
    return jax.shard_map(
        body,
        mesh=mesh,
        in_specs=(
            P("rep", None, "shard", None),
            P("rep", None, "shard", None),
            P("rep", "shard", None),
            P("rep", None, "shard", None),
            P("rep", None, "shard", None),
            P("rep", "shard", None),
            P(None, "shard", None),
            P(None, "shard", None),
            P("shard", None),
            P(None, "shard", None),
            P(None, "shard", None),
            P("shard", None),
            P(),
            P(None, "shard"),
            P(None, "shard"),
            P("rep", None, "shard"),
        ),
        out_specs=(
            P(None, "shard", None),
            P(None, "shard", None),
            P("shard", None),
            P(None, "shard", None),
            P(None, "shard", None),
            P("shard", None),
            P("rep", None, "shard", None),
            P("rep", None, "shard", None),
            P("rep", "shard", None),
            P(None, "shard", None),
            P(None, "shard", None),
            P("shard", None),
            P(),
            P(None, "shard"),
            P(None, "shard"),
        ),
        check_vma=False,
    )
```

profile of v0, /device:TPU:1, one launch (start us, length us, event | category | flops | bytes accessed | tf_op | source)
XLA Modules:
  0.0 417.3 jit_solution(11912199704461353907)
XLA Ops:
  7.2 1.3 copy.47
  8.6 2.7 convolution_bitcast_fusion.2
  11.3 2.2 convolution_bitcast_fusion.3
  13.5 2.6 convolution_bitcast_fusion
  16.2 41.9 %all-reduce.6.cloned.1.call-done = (f32[32,256]{1,0:T(8,128)}, f32[2,32,96]{2,1,0:T(8,128)}, f32[8,32,24]{1,2,0:T(8,128)}, f32[3,24]{1,0:T(4,128)}) async-done(((f32[32,256]{1,0:T(8,128)}, f32[2,32,96]{2,1,0:T(8,128)}, f32[8,32,24]{1,2,0:T(8,128)}, f32[3,24]{1,0:T(4,128)}), (f32[32,256]{1,0:T(8,128)}, f32[2,32,96]{2,1,0:T(8,128)}, f32[8,32,24]{1,2,0:T(8,128)}, ...) | async-done | bytes 82224 | tf_op jit(solution)/shard_map/psum | solution.py:46
  58.2 1.0 convolution_bitcast_fusion.4
  59.2 1.0 fusion.35
  60.2 1.4 fusion.25
  61.6 125.0 %psum.45 = f32[11,32,32]{1,2,0:T(8,128)S(1)} all-reduce(f32[11,32,32]{1,2,0:T(8,128)S(1)} %pad_maximum_fusion.1), channel_id=1, replica_groups=mesh['rep'=4,'shard'=32] {'shard'}, use_global_device_ids=true, to_apply=%region_3.0 | all-reduce | flops 11264 | bytes 90112 | tf_op jit(solution)/shard_map/psum | solution.py:60
  186.7 0.7 fusion.19
  187.4 32.9 %custom-call.7 = f32[11,32,32]{2,1,0:T(8,128)S(1)} custom-call(f32[11,32,32]{2,1,0:T(8,128)} %fusion.19), custom_call_target="Cholesky" | custom-call | tf_op jit(solution)/shard_map/jit(cholesky)/cholesky | solution.py:8
  220.6 27.1 %custom-call.8 = f32[11,1,32,32]{2,3,1,0:T(8,128)S(1)} custom-call(f32[11,1,32,32]{3,2,1,0:T(8,128)S(1)} %select_bitcast_fusion), custom_call_target="InvertDiagBlocksLowerTriangular" | custom-call | tf_op jit(solution)/shard_map/triangular_solve | solution.py:10
  248.5 0.9 fusion.30
  249.5 0.9 fusion.33
  250.4 0.6 convolution_bitcast_fusion.1
  251.5 0.8 fusion.10
  252.3 1.1 pad_maximum_fusion
  253.4 0.7 copy-done.14
  254.1 0.6 multiply_subtract_fusion.3
  254.7 147.5 %all-reduce.4.cloned.1.call-done = f32[11,32,768]{2,1,0:T(8,128)} async-done(((f32[11,32,768]{2,1,0:T(8,128)}), f32[11,32,768]{2,1,0:T(8,128)}) %all-reduce.4.cloned.1.call-update) | async-done | bytes 1081360 | tf_op jit(solution)/shard_map/psum | solution.py:73
  402.2 1.4 broadcast_multiply_fusion
  403.7 2.1 fusion.50
  405.8 2.1 fusion.49
  407.9 2.5 fusion.48
  (48 shorter events, 2.0 us)
Async XLA Ops:
  7.2 4.1 copy-start.2
  7.2 4.1 copy-start.6
  7.2 51.0 %all-reduce.6.cloned.1.call-start = ((), (), s32[]{:S(2)}) async-start(), calls=%async_computation.1 | async-start | bytes 331776 | tf_op jit(solution)/shard_map/psum | solution.py:46
  8.6 4.9 %copy-start.1 = (f32[1,8,24,768]{3,2,1,0:T(8,128)S(1)}, f32[1,8,24,768]{3,2,1,0:T(8,128)}, u32[]{:S(2)}) copy-start(f32[1,8,24,768]{3,2,1,0:T(8,128)} %param.19) | copy-start | bytes 1769476
  8.6 4.9 %copy-start.5 = (bf16[1,8,24,768]{3,2,1,0:T(8,128)(2,1)S(1)}, bf16[1,8,24,768]{3,2,1,0:T(8,128)(2,1)}, u32[]{:S(2)}) copy-start(bf16[1,8,24,768]{3,2,1,0:T(8,128)(2,1)} %param.16) | copy-start | bytes 884740
  16.1 386.0 %all-reduce.4.cloned.1.call-start = ((), (), s32[]{:S(2)}) async-start(), calls=%async_computation | async-start | bytes 2162688 | tf_op jit(solution)/shard_map/psum | solution.py:73
  61.6 186.6 %copy-start.13 = (f32[8,32,24]{1,2,0:T(8,128)S(1)}, f32[8,32,24]{1,2,0:T(8,128)}, u32[]{:S(2)}) copy-start(f32[8,32,24]{1,2,0:T(8,128)} %get-tuple-element.17) | copy-start | bytes 73732
  186.7 63.7 %copy-start = (f32[1,256,768]{2,1,0:T(8,128)S(1)}, f32[1,256,768]{2,1,0:T(8,128)}, u32[]{:S(2)}) copy-start(f32[1,256,768]{2,1,0:T(8,128)} %param.21) | copy-start | bytes 2359300
  186.7 63.7 %copy-start.4 = (bf16[1,256,768]{2,1,0:T(8,128)(2,1)S(1)}, bf16[1,256,768]{2,1,0:T(8,128)(2,1)}, u32[]{:S(2)}) copy-start(bf16[1,256,768]{2,1,0:T(8,128)(2,1)} %param.18) | copy-start | bytes 1179652
  253.4 0.7 copy-start.14
  253.4 0.7 copy-start.15
  253.4 0.7 copy-start.16
  402.2 1.4 copy-start.9
  402.2 1.6 copy-start.10
  403.7 4.2 %copy-start.3 = (f32[11,32,768]{2,1,0:T(8,128)}, f32[11,32,768]{2,1,0:T(8,128)S(1)}, u32[]{:S(2)}) copy-start(f32[11,32,768]{2,1,0:T(8,128)S(1)} %broadcast_multiply_fusion) | copy-start | bytes 3244036
  403.7 2.1 copy-start.11
  403.7 2.1 copy-start.12
  405.8 2.1 copy-start.7
  405.8 2.1 copy-start.8
Sparse Core Ops, SparseCore 0:
  16.3 41.8 all-reduce.5
  253.5 148.5 all-reduce.3
where the time goes:
time: 418 us; the launch traced here: 417 us
  waiting for transfers between devices  189 us (45%)
  blocking collectives  125 us (30%)
  other arithmetic  64.1 us (15%)
  matrix products  22.1 us (5%)
  between operations  14.3 us (3%)
    psum x1, waiting for transfers between devices, body(): next_start = lax.psum(partial_right, ('rep', 'shard')) / replicas  147 us
    psum x1, blocking collectives, body(): grams = lax.psum(local_grams, 'shard')  125 us
    psum x1, waiting for transfers between devices, body(): lax.psum((proj_attention, proj_dense, proj_embedding), 'rep')  41.9 us
    another operation x4, other arithmetic, invert(): factor = jnp.linalg.cholesky(grams)  33.1 us
    another operation x3, other arithmetic, invert(): lax.linalg.triangular_solve(factor, identity, left_side=True, lower=True)  27.2 us
  transfers between devices with their start and end apart: 2, of which 2 were waited for; matrix products, arithmetic and copies ran while one was open for 0% of the time, Pallas kernels for 0%

commit v1 on v0

v1 whole, which is shorter than its diff:
```python
import jax
import jax.numpy as jnp
from jax import lax
from jax.experimental import pallas as pl
from jax.experimental.pallas import tpu as pltpu
from jax.sharding import PartitionSpec as P

MESH = pl.DeviceIdType.MESH
F32, BF16 = jnp.float32, jnp.bfloat16
D = 768
HALF = 384
RANK = 32
NMAT = 11
LEFT = NMAT * RANK
ROWS = 640
AD_ROWS = 384
AD_LEFT = 10 * RANK
NT = (((1,), (1,)), ((), ()))
NN = (((1,), (0,)), ((), ()))
TN = (((0,), (0,)), ((), ()))


def split(x):
    hi = x.astype(BF16)
    return hi, (x - hi.astype(F32)).astype(BF16)


def dot(a, b, dims):
    return lax.dot_general(a, b, dims, preferred_element_type=F32)


def dot3(a, b, dims):
    (ah, al), (bh, bl) = a, b
    return dot(ah, bh, dims) + (dot(al, bh, dims) + dot(ah, bl, dims))


def exact(a, b, dims):
    return lax.dot_general(a, b, dims, preferred_element_type=F32, precision=lax.Precision.HIGHEST)


def row_mask(lefts, rows):
    m = lax.broadcasted_iota(jnp.int32, (lefts, rows), 0) // RANK
    r = lax.broadcasted_iota(jnp.int32, (lefts, rows), 1)
    low = jnp.where(m < 8, 24 * m, jnp.where(m < 10, 96 * m - 576, AD_ROWS))
    high = low + jnp.where(m < 8, 24, jnp.where(m < 10, 96, 256))
    return (r >= low) & (r < high)


def fold(x, blocks):
    total = x[:RANK]
    for m in range(1, blocks):
        total = total + x[m * RANK : (m + 1) * RANK]
    return total


def position():
    x, s = lax.axis_index("rep"), lax.axis_index("shard")
    return x, s // 2, s % 2


def device(x, plane, core):
    return (x, plane * 2 + core)


def exchange_kernel(
    ag_hbm, dg_hbm, eg_hbm, ae_hbm, de_hbm, ee_hbm, warm_hbm, norm_ref,
    right_hbm, left_hbm, norm_out,
    ag, dg, eg, ae, de, ee, warm, merged_hi, merged_lo,
    left_a, left_b, left_sum, other, own, sibling, slots, right, norm_slots,
    in_sem, left_send, left_recv, core_send, core_recv, rs_send, rs_recv,
    ag_send, ag_recv, half_send, half_recv, norm_send, norm_recv, out_sem,
):
    x, plane, core = position()
    chip = x * 16 + plane
    here = (plane * 11) % 16
    owner = here < NMAT

    barrier = pltpu.get_barrier_semaphore()
    pl.semaphore_signal(barrier, inc=1, device_id=device(x, plane, 1 - core), device_id_type=MESH)
    for d in range(1, 4):
        pl.semaphore_signal(barrier, inc=1, device_id=device((x + d) % 4, plane, core), device_id_type=MESH)

    def greet(i, carry):
        pl.semaphore_signal(barrier, inc=1, device_id=device(x, (plane + i) % 16, core), device_id_type=MESH)
        return carry

    lax.fori_loop(1, 16, greet, 0)

    loads = [
        pltpu.make_async_copy(a, b, in_sem.at[i])
        for i, (a, b) in enumerate(
            [(warm_hbm, warm), (ag_hbm, ag), (ae_hbm, ae), (dg_hbm, dg), (de_hbm, de), (eg_hbm, eg), (ee_hbm, ee)]
        )
    ]
    for copy in loads:
        copy.start()

    def put(row, rows, value):
        hi, lo = split(value)
        for h in range(2):
            merged_hi[h, row : row + rows, :] = hi[:, h * HALF : (h + 1) * HALF]
            merged_lo[h, row : row + rows, :] = lo[:, h * HALF : (h + 1) * HALF]

    norm_slots[x] = jnp.zeros((8, 128), F32)
    norm_slots[x, 0:3, 0:24] = norm_ref[0]

    loads[0].wait()
    loads[1].wait()
    loads[2].wait()
    for m in range(0, 8, 2):
        put(24 * m, 48, jnp.concatenate(
            [ag[0, m].astype(F32) + ae[0, m], ag[0, m + 1].astype(F32) + ae[0, m + 1]], 0))
    loads[3].wait()
    loads[4].wait()
    for m in range(2):
        put(192 + 96 * m, 96, dg[0, m].astype(F32) + de[0, m])

    def project(first, last, row, rows, mask):
        w = split(warm[first:last].reshape((last - first) * RANK, D))
        total = None
        for h in range(2):
            part = dot3(
                [p[:, h * HALF : (h + 1) * HALF] for p in w],
                (merged_hi[h, row : row + rows, :], merged_lo[h, row : row + rows, :]),
                NT,
            )
            total = part if total is None else total + part
        if mask is not None:
            total = fold(jnp.where(mask, total, 0.0), last - first)
        return total

    mask = row_mask(AD_LEFT, AD_ROWS)
    left_a[x] = project(0, 10, 0, AD_ROWS, mask)

    pl.semaphore_wait(barrier, 19)

    def share(buf, i):
        return [
            pltpu.make_async_remote_copy(
                src_ref=buf.at[x], dst_ref=buf.at[x], send_sem=left_send.at[i, d - 1], recv_sem=left_recv.at[i, d - 1],
                device_id=device((x + d) % 4, plane, core), device_id_type=MESH)
            for d in range(1, 4)
        ]

    share_a = share(left_a, 0)
    for copy in share_a:
        copy.start()
    loads[5].wait()
    loads[6].wait()
    for m in range(2):
        put(AD_ROWS + 128 * m, 128, eg[0, 128 * m : 128 * m + 128].astype(F32) + ee[0, 128 * m : 128 * m + 128])
    left_b[x] = project(10, 11, AD_ROWS, 256, None)
    share_b = share(left_b, 1)
    for copy in share_b:
        copy.start()
    share_n = [
        pltpu.make_async_remote_copy(
            src_ref=norm_slots.at[x], dst_ref=norm_slots.at[x], send_sem=norm_send.at[d - 1], recv_sem=norm_recv.at[d - 1],
            device_id=device((x + d) % 4, plane, core), device_id_type=MESH)
        for d in range(1, 4)
    ]
    for copy in share_n:
        copy.start()

    def contract(left, half, row, rows):
        return dot3(left, (merged_hi[half, row : row + rows, :], merged_lo[half, row : row + rows, :]), NN)

    def swap(i, row, rows):
        return pltpu.make_async_remote_copy(
            src_ref=other.at[row : row + rows], dst_ref=sibling.at[row : row + rows], send_sem=core_send.at[i],
            recv_sem=core_recv.at[i], device_id=device(x, plane, 1 - core), device_id_type=MESH)

    for copy in share_a:
        copy.wait_recv()
    pa = (left_a[0] + left_a[1] + left_a[2] + left_a[3]) * 0.25
    left_sum[:, 0:AD_ROWS] = pa
    spread = split(jnp.where(mask, jnp.concatenate([pa] * 10, 0), 0.0))
    other[0:AD_LEFT, :] = contract(spread, 1 - core, 0, AD_ROWS)
    swap_a = swap(0, 0, AD_LEFT)
    swap_a.start()
    own[0:AD_LEFT, :] = contract(spread, core, 0, AD_ROWS)

    for copy in share_b:
        copy.wait_recv()
    pb = (left_b[0] + left_b[1] + left_b[2] + left_b[3]) * 0.25
    left_sum[:, AD_ROWS:ROWS] = pb
    pb = split(pb)
    other[AD_LEFT:LEFT, :] = contract(pb, 1 - core, AD_ROWS, 256)
    swap_b = swap(1, AD_LEFT, RANK)
    swap_b.start()
    own[AD_LEFT:LEFT, :] = contract(pb, core, AD_ROWS, 256)
    left_out = pltpu.make_async_copy(left_sum, left_hbm, out_sem.at[0])
    left_out.start()

    swap_a.wait_recv()
    own[0:AD_LEFT, :] = own[0:AD_LEFT, :] + sibling[0:AD_LEFT, :]

    def scatter(i, carry):
        to_x = (x + 2 + i) % 4
        m = i // 4
        to_plane = (3 * m) % 16

        @pl.when((to_x != x) | (to_plane != plane))
        def _():
            pltpu.make_async_remote_copy(
                src_ref=own.at[pl.ds(pl.multiple_of(RANK * m + 8 * to_x, 8), 8)], dst_ref=slots.at[chip], send_sem=rs_send,
                recv_sem=rs_recv, device_id=device(to_x, to_plane, core), device_id_type=MESH).start()

        return carry

    lax.fori_loop(0, 40, scatter, 0)
    swap_b.wait_recv()
    own[AD_LEFT:LEFT, :] = own[AD_LEFT:LEFT, :] + sibling[AD_LEFT:LEFT, :]
    lax.fori_loop(40, 44, scatter, 0)

    @pl.when(owner)
    def _():
        mine = pl.ds(pl.multiple_of(RANK * here + 8 * x, 8), 8)
        slots[chip] = own[mine, :]
        pltpu.make_async_copy(slots.at[0:63], slots.at[0:63], rs_recv).wait()

        def add(i, total):
            return total + slots[i]

        total = lax.fori_loop(1, 64, add, slots[0])
        right[core, mine, :] = total * 0.25

        def gather(i, carry):
            to = (chip + i) % 64
            pltpu.make_async_remote_copy(
                src_ref=right.at[core, mine], dst_ref=right.at[core, mine], send_sem=ag_send,
                recv_sem=ag_recv, device_id=device(to // 16, to % 16, core), device_id_type=MESH).start()
            return carry

        lax.fori_loop(1, 64, gather, 0)
        pltpu.make_async_copy(own.at[0 : LEFT - 8], own.at[0 : LEFT - 8], ag_recv).wait()

    @pl.when(jnp.logical_not(owner))
    def _():
        pltpu.make_async_copy(own, own, ag_recv).wait()

    forward = pltpu.make_async_remote_copy(
        src_ref=right.at[core], dst_ref=right.at[core], send_sem=half_send, recv_sem=half_recv,
        device_id=device(x, plane, 1 - core), device_id_type=MESH)
    forward.start()
    out_own = pltpu.make_async_copy(right.at[core], right_hbm.at[core], out_sem.at[1])
    out_own.start()
    for copy in share_n:
        copy.wait_recv()
    norm_out[...] = norm_slots[0] + norm_slots[1] + norm_slots[2] + norm_slots[3]
    forward.wait_recv()
    out_other = pltpu.make_async_copy(right.at[1 - core], right_hbm.at[1 - core], out_sem.at[2])
    out_other.start()

    for copy in share_a + share_b + share_n + [swap_a, swap_b, forward]:
        copy.wait_send()

    @pl.when(owner)
    def _():
        pltpu.make_async_copy(own.at[0 : LEFT - 8], own.at[0 : LEFT - 8], rs_send).wait()
        pltpu.make_async_copy(slots.at[0:63], slots.at[0:63], ag_send).wait()

    @pl.when(jnp.logical_not(owner))
    def _():
        pltpu.make_async_copy(own, own, rs_send).wait()

    left_out.wait()
    out_own.wait()
    out_other.wait()


def invert(gram):
    lane = lax.broadcasted_iota(jnp.int32, (8, 128), 1)
    column = lane % RANK
    base = lane - column
    sub = lax.broadcasted_iota(jnp.int32, (8, 128), 0)
    a = [[gram[8 * g : 8 * g + 8, 128 * l : 128 * l + 128] for l in range(3)] for g in range(4)]
    for p in range(RANK):
        gp, sp = p // 8, p % 8
        for l in range(3):
            index = base + p
            pick = [jnp.take_along_axis(a[g][l], index, axis=1) for g in range(gp, 4)]
            pivot = pick[0][sp : sp + 1, :]
            row = jnp.where(column[:1] == p, 1.0, a[gp][l][sp : sp + 1, :]) / pivot
            for g in range(gp, 4):
                f = pick[g - gp]
                keep = jnp.where(column == p, 0.0, a[g][l])
                new = keep - f * row
                a[g][l] = jnp.where(sub > sp, new, a[g][l]) if g == gp else new
    out = []
    for g in range(4):
        parts = []
        for l in range(3):
            i = sub + 8 * g
            pivot = jnp.take_along_axis(a[g][l], base + i, axis=1)
            value = jnp.where(column < i, a[g][l], jnp.where(column == i, 1.0, 0.0))
            parts.append(value / jnp.sqrt(pivot))
        out.append(jnp.concatenate(parts, 1))
    return jnp.concatenate(out, 0)


def finish_kernel(
    ag_hbm, dg_hbm, eg_hbm, ae_hbm, de_hbm, ee_hbm, aw_hbm, dw_hbm, ew_hbm, am_hbm, dm_hbm, em_hbm,
    warm_hbm, right_hbm, left_hbm, norm_total, norm_scale, norm_momentum,
    au_hbm, du_hbm, eu_hbm, ac_hbm, dc_hbm, ec_hbm, ar_hbm, dr_hbm, er_hbm, av_hbm, dv_hbm, ev_hbm,
    next_hbm, norm_updated, norm_velocity,
    ag, dg, eg, ae, de, ee, aw, dw, ew, am, dm, em, warm, right, left,
    au, du, eu, ac, dc, ec, ar, dr, er, av, dv, ev, start, wide, in_sem, out_sem,
):
    pairs = [
        (right_hbm, right), (warm_hbm, warm), (left_hbm, left),
        (ag_hbm, ag), (ae_hbm, ae), (am_hbm, am), (aw_hbm, aw),
        (dg_hbm, dg), (de_hbm, de), (dm_hbm, dm), (dw_hbm, dw),
        (eg_hbm, eg), (ee_hbm, ee), (em_hbm, em), (ew_hbm, ew),
    ]
    loads = [pltpu.make_async_copy(a, b, in_sem.at[i]) for i, (a, b) in enumerate(pairs)]
    for copy in loads:
        copy.start()

    velocity = 0.9 * norm_momentum[...] + norm_total[0:3, 0:24] / 4
    norm_velocity[...] = velocity
    norm_updated[...] = norm_scale[...] - 0.05 * velocity

    wide[LEFT:, :] = jnp.zeros((32, D), F32)
    loads[0].wait()
    loads[1].wait()
    wide[0:LEFT, :] = warm[...].reshape(LEFT, D)
    gram = exact(right[0], wide[:, 0:HALF], NT) + exact(right[1], wide[:, HALF:D], NT)
    mi = lax.broadcasted_iota(jnp.int32, (LEFT, HALF), 0) // RANK
    mj = lax.broadcasted_iota(jnp.int32, (LEFT, HALF), 1) // RANK
    same = mi == mj
    gram = fold(jnp.where(same, gram, 0.0), NMAT)
    i = lax.broadcasted_iota(jnp.int32, (RANK, HALF), 0)
    j = lax.broadcasted_iota(jnp.int32, (RANK, HALF), 1)
    gram = jnp.where(j < LEFT, gram, jnp.where(i == j - LEFT, 1.0, 0.0))
    inverse = invert(gram)
    inverse = jnp.where(same, jnp.concatenate([inverse] * NMAT, 0), 0.0)[:, 0:LEFT]
    for h in range(2):
        start[:, h * HALF : (h + 1) * HALF] = exact(inverse, right[h], NN)
    copies = []

    def send(src, dst):
        copy = pltpu.make_async_copy(src, dst, out_sem.at[len(copies)])
        copy.start()
        copies.append(copy)

    send(start, next_hbm)
    loads[2].wait()
    spread = jnp.where(row_mask(LEFT, ROWS), jnp.concatenate([left[...]] * NMAT, 0), 0.0)
    ortho = exact(inverse, spread, NN)
    oh, ol = split(ortho)
    oh, ol = oh.T, ol.T
    sh, sl = split(start[...])

    def approx(row, rows):
        part = slice(row, row + rows)
        return dot3((oh[part], ol[part]), (sh, sl), NN)

    def write(value, g, e, w, m, u, c, r, v):
        r[...] = g[...].astype(F32) + e[...] - value
        velocity = 0.9 * m[...] + value
        updated = w[...] - 0.05 * velocity
        v[...] = velocity
        u[...] = updated
        c[...] = updated.astype(BF16)

    for k in range(3, 7):
        loads[k].wait()
    value = approx(0, 192)
    for m in range(8):
        write(value[24 * m : 24 * m + 24], ag.at[0, m], ae.at[0, m], aw.at[m], am.at[m],
              au.at[m], ac.at[m], ar.at[0, m], av.at[m])
    for a, b in ((au, au_hbm), (ac, ac_hbm), (ar, ar_hbm), (av, av_hbm)):
        send(a, b)
    for k in range(7, 11):
        loads[k].wait()
    for m in range(2):
        write(approx(192 + 96 * m, 96), dg.at[0, m], de.at[0, m], dw.at[m], dm.at[m],
              du.at[m], dc.at[m], dr.at[0, m], dv.at[m])
    for a, b in ((du, du_hbm), (dc, dc_hbm), (dr, dr_hbm), (dv, dv_hbm)):
        send(a, b)
    for k in range(11, 15):
        loads[k].wait()
    for m in range(2):
        part = pl.ds(128 * m, 128)
        write(approx(AD_ROWS + 128 * m, 128), eg.at[0, part], ee.at[0, part], ew.at[part], em.at[part],
              eu.at[part], ec.at[part], er.at[0, part], ev.at[part])
        for a, b in ((eu, eu_hbm), (ec, ec_hbm), (ev, ev_hbm)):
            send(a.at[part], b.at[part])
        send(er.at[0, part], er_hbm.at[0, part])
    for copy in copies:
        copy.wait()


ANY = pl.BlockSpec(memory_space=pl.ANY)
VMEM = pl.BlockSpec(memory_space=pltpu.VMEM)
DMA = pltpu.SemaphoreType.DMA


def body(
    attention_grad, dense_grad, embedding_grad, attention_error, dense_error, embedding_error,
    attention_weight, dense_weight, embedding_weight, attention_momentum, dense_momentum, embedding_momentum,
    warm_start, norm_scale, norm_momentum, norm_grad,
):
    grads = [attention_grad, dense_grad, embedding_grad]
    errors = [attention_error, dense_error, embedding_error]
    weights = [attention_weight, dense_weight, embedding_weight]
    momenta = [attention_momentum, dense_momentum, embedding_momentum]

    def like(arrays, dtype=None):
        return [pltpu.VMEM(a.shape, dtype or a.dtype) for a in arrays]

    right, left, norm_total = pl.pallas_call(
        exchange_kernel,
        name="exchange",
        out_shape=(
            jax.ShapeDtypeStruct((2, LEFT, HALF), F32),
            jax.ShapeDtypeStruct((RANK, ROWS), F32),
            jax.ShapeDtypeStruct((8, 128), F32),
        ),
        in_specs=[ANY] * 7 + [VMEM],
        out_specs=(ANY, ANY, VMEM),
        scratch_shapes=like(grads) + like(errors) + like([warm_start]) + [
            pltpu.VMEM((2, ROWS, HALF), BF16),
            pltpu.VMEM((2, ROWS, HALF), BF16),
            pltpu.VMEM((4, RANK, AD_ROWS), F32),
            pltpu.VMEM((4, RANK, 256), F32),
            pltpu.VMEM((RANK, ROWS), F32),
            pltpu.VMEM((LEFT, HALF), F32),
            pltpu.VMEM((LEFT, HALF), F32),
            pltpu.VMEM((LEFT, HALF), F32),
            pltpu.VMEM((64, 8, HALF), F32),
            pltpu.VMEM((2, LEFT, HALF), F32),
            pltpu.VMEM((4, 8, 128), F32),
            DMA((7,)), DMA((2, 3)), DMA((2, 3)), DMA((2,)), DMA((2,)), DMA, DMA,
            DMA, DMA, DMA, DMA, DMA((3,)), DMA((3,)), DMA((3,)),
        ],
        compiler_params=pltpu.CompilerParams(collective_id=0, has_side_effects=True, vmem_limit_bytes=40 << 20),
    )(*grads, *errors, warm_start, norm_grad)

    shapes = [
        *[jax.ShapeDtypeStruct(a.shape, F32) for a in weights],
        *[jax.ShapeDtypeStruct(a.shape, BF16) for a in weights],
        *[jax.ShapeDtypeStruct(a.shape, F32) for a in errors],
        *[jax.ShapeDtypeStruct(a.shape, F32) for a in weights],
        jax.ShapeDtypeStruct((LEFT, D), F32),
        jax.ShapeDtypeStruct(norm_scale.shape, F32),
        jax.ShapeDtypeStruct(norm_scale.shape, F32),
    ]
    outs = pl.pallas_call(
        finish_kernel,
        name="finish",
        out_shape=tuple(shapes),
        in_specs=[ANY] * 15 + [VMEM] * 3,
        out_specs=tuple([ANY] * 13 + [VMEM] * 2),
        scratch_shapes=like(grads) + like(errors) + like(weights) + like(momenta) + like([warm_start, right, left])
        + like(weights) + like(weights, BF16) + like(errors) + like(weights) + [
            pltpu.VMEM((LEFT, D), F32), pltpu.VMEM((HALF, D), F32), DMA((15,)), DMA((17,)),
        ],
        compiler_params=pltpu.CompilerParams(vmem_limit_bytes=40 << 20),
    )(*grads, *errors, *weights, *momenta, warm_start, right, left, norm_total, norm_scale, norm_momentum)
    outs = list(outs)
    outs[12] = outs[12].reshape(NMAT, RANK, D)
    return tuple(outs)


def solution(mesh):
    matrices = (P(None, "shard", None), P(None, "shard", None), P("shard", None))
    replicas = (P("rep", None, "shard", None), P("rep", None, "shard", None), P("rep", "shard", None))
    norm = P(None, "shard")
    return jax.shard_map(
        body,
        mesh=mesh,
        in_specs=replicas + replicas + matrices + matrices + (P(), norm, norm, P("rep", None, "shard")),
        out_specs=matrices + matrices + replicas + matrices + (P(), norm, norm),
        check_vma=False,
    )
```

time: 418 us -> 69.4 us (0.17)
  waiting for transfers between devices: 189 us -> 0 us
  blocking collectives: 125 us -> 0 us
  other arithmetic: 64.1 us -> 0 us
  Pallas kernels: 0 us -> 59.9 us
  matrix products: 22.1 us -> 0 us
  between operations: 14.3 us -> 0.92 us
  local copies, waits for them, and re-layouts: 2.29 us -> 8.14 us
    psum x2 -> x0, waiting for transfers between devices: 189 us -> none  [the longest x1 147 us: body(): next_start = lax.psum(partial_right, ('rep', 'shard')) / replicas]
    psum x1 -> x0, blocking collectives: 125 us -> none  [body(): grams = lax.psum(local_grams, 'shard')]
    another operation x7 -> x0, other arithmetic: 60.3 us -> none  [the longest x4 33.1 us: invert(): factor = jnp.linalg.cholesky(grams)]
    pallas_call x0 -> x2, Pallas kernels: none -> 59.9 us  [the longest x1 43.1 us: body(): pl.pallas_call(exchange_kernel, name='exchange', out_shape=(jax.ShapeDtyp...]
    dot_general x15 -> x0, matrix products: 21.6 us -> none  [the longest x1 2.73 us: body(): jnp.einsum('kc,rc->kr', warm_start[10], merged_embedding, precision=highest)]
    unnamed x35 -> x31, local copies, waits for them, and re-layouts: 2.18 us -> 8.14 us
  transfers between devices with their start and end apart: 2 -> 0, of which waited for: 2 -> 0; matrix products, arithmetic and copies ran while one was open for 0% -> 0% of each run, Pallas kernels for 0% -> 0%
where the time goes in v1:
time: 69.4 us; the launch traced here: 69 us
  Pallas kernels  59.9 us (86%)
  local copies, waits for them, and re-layouts  8.14 us (12%)
  between operations  0.92 us (1%)
    pallas_call x1, Pallas kernels, body(): pl.pallas_call(exchange_kernel, name='exchange', out_shape=(jax.ShapeDtyp...  43.1 us
    pallas_call x1, Pallas kernels, body(): pl.pallas_call(finish_kernel, name='finish', out_shape=tuple(shapes), in_...  16.8 us
    unnamed x31, local copies, waits for them, and re-layouts  8.14 us

profile of v1, /device:TPU:1, one launch (start us, length us, event | category | flops | bytes accessed | tf_op | source)
XLA Modules:
  0.0 69.0 jit_solution(16116007622399511711)
XLA Ops:
  0.6 0.7 copy.31.norm_ref
  1.3 0.0 copy-start
  1.3 1.2 %copy-done = f32[11,32,768]{2,1,0:T(8,128)S(1)} copy-done((f32[11,32,768]{2,1,0:T(8,128)S(1)}, f32[11,32,768]{2,1,0:T(8,128)}, u32[]{:S(2)}) %copy-start) | copy-done | bytes 1081368
  2.6 0.0 copy-start.1
  2.6 1.1 %copy-done.1 = f32[1,256,768]{2,1,0:T(8,128)S(1)} copy-done((f32[1,256,768]{2,1,0:T(8,128)S(1)}, f32[1,256,768]{2,1,0:T(8,128)}, u32[]{:S(2)}) %copy-start.1) | copy-done | bytes 786456
  3.7 1.1 %copy-done.2 = f32[1,8,24,768]{3,2,1,0:T(8,128)S(1)} copy-done((f32[1,8,24,768]{3,2,1,0:T(8,128)S(1)}, f32[1,8,24,768]{3,2,1,0:T(8,128)}, u32[]{:S(2)}) %copy-start.2) | copy-done | bytes 589848
  4.8 1.1 %copy-done.3 = f32[1,2,96,768]{3,2,1,0:T(8,128)S(1)} copy-done((f32[1,2,96,768]{3,2,1,0:T(8,128)S(1)}, f32[1,2,96,768]{3,2,1,0:T(8,128)}, u32[]{:S(2)}) %copy-start.3) | copy-done | bytes 589848
  5.8 1.0 %copy-done.4 = bf16[1,256,768]{2,1,0:T(8,128)(2,1)S(1)} copy-done((bf16[1,256,768]{2,1,0:T(8,128)(2,1)S(1)}, bf16[1,256,768]{2,1,0:T(8,128)(2,1)}, u32[]{:S(2)}) %copy-start.4) | copy-done | bytes 393240
  6.8 1.0 %copy-done.5 = bf16[1,8,24,768]{3,2,1,0:T(8,128)(2,1)S(1)} copy-done((bf16[1,8,24,768]{3,2,1,0:T(8,128)(2,1)S(1)}, bf16[1,8,24,768]{3,2,1,0:T(8,128)(2,1)}, u32[]{:S(2)}) %copy-start.5) | copy-done | bytes 294936
  7.8 1.0 %copy-done.6 = bf16[1,2,96,768]{3,2,1,0:T(8,128)(2,1)S(1)} copy-done((bf16[1,2,96,768]{3,2,1,0:T(8,128)(2,1)S(1)}, bf16[1,2,96,768]{3,2,1,0:T(8,128)(2,1)}, u32[]{:S(2)}) %copy-start.6) | copy-done | bytes 294936
  8.8 0.0 copy-start.11
  8.8 0.0 copy-start.12
  8.8 0.0 copy-start.13
  8.8 0.0 copy-start.14
  8.8 43.1 %exchange.1 = (f32[2,352,384]{2,1,0:T(8,128)S(1)}, f32[32,640]{1,0:T(8,128)S(1)}, f32[8,128]{1,0:T(8,128)S(1)}) custom-call(bf16[1,8,24,768]{3,2,1,0:T(8,128)(2,1)S(1)} %copy-done.5, bf16[1,2,96,768]{3,2,1,0:T(8,128)(2,1)S(1)} %copy-done.6, bf16[1,256,768]{2,1,0:T(8,128)(2,1)S(1)} %copy-done.4, f32[1,8,24,768]{3,2,1,0:T(8,128)S(1)} %copy-done.2, ...), custom_call_target="tpu_custom_call" | custom-call | tf_op jit(solution)/shard_map/exchange/pallas_call | solution.py:413
  51.9 0.0 copy-done.7
  51.9 0.0 copy-done.8
  51.9 0.0 copy-done.9
  51.9 0.0 copy-done.10
  52.0 0.0 copy-done.11
  52.0 0.0 copy-done.12
  52.0 0.0 copy-done.13
  52.0 0.0 copy-done.14
  52.0 16.8 %finish.1 = (f32[8,24,768]{2,1,0:T(8,128)}, f32[2,96,768]{2,1,0:T(8,128)}, f32[256,768]{1,0:T(8,128)}, bf16[8,24,768]{2,1,0:T(8,128)(2,1)}, bf16[2,96,768]{2,1,0...) custom-call(bf16[1,8,24,768]{3,2,1,0:T(8,128)(2,1)S(1)} %copy-done.5, ...), custom_call_target="tpu_custom_call" | custom-call | tf_op jit(solution)/shard_map/finish/pallas_call | solution.py:450
  (9 shorter events, 0.0 us)
Async XLA Ops:
  1.3 1.2 %copy-start = (f32[11,32,768]{2,1,0:T(8,128)S(1)}, f32[11,32,768]{2,1,0:T(8,128)}, u32[]{:S(2)}) copy-start(f32[11,32,768]{2,1,0:T(8,128)} %warm_hbm.3) | copy-start | bytes 3244036
  2.6 1.1 %copy-start.1 = (f32[1,256,768]{2,1,0:T(8,128)S(1)}, f32[1,256,768]{2,1,0:T(8,128)}, u32[]{:S(2)}) copy-start(f32[1,256,768]{2,1,0:T(8,128)} %ee_hbm.3) | copy-start | bytes 2359300
  3.7 1.1 %copy-start.2 = (f32[1,8,24,768]{3,2,1,0:T(8,128)S(1)}, f32[1,8,24,768]{3,2,1,0:T(8,128)}, u32[]{:S(2)}) copy-start(f32[1,8,24,768]{3,2,1,0:T(8,128)} %ae_hbm.3) | copy-start | bytes 1769476
  4.8 1.1 %copy-start.3 = (f32[1,2,96,768]{3,2,1,0:T(8,128)S(1)}, f32[1,2,96,768]{3,2,1,0:T(8,128)}, u32[]{:S(2)}) copy-start(f32[1,2,96,768]{3,2,1,0:T(8,128)} %de_hbm.3) | copy-start | bytes 1769476
  5.8 1.0 %copy-start.4 = (bf16[1,256,768]{2,1,0:T(8,128)(2,1)S(1)}, bf16[1,256,768]{2,1,0:T(8,128)(2,1)}, u32[]{:S(2)}) copy-start(bf16[1,256,768]{2,1,0:T(8,128)(2,1)} %eg_hbm.3) | copy-start | bytes 1179652
  6.8 1.0 %copy-start.5 = (bf16[1,8,24,768]{3,2,1,0:T(8,128)(2,1)S(1)}, bf16[1,8,24,768]{3,2,1,0:T(8,128)(2,1)}, u32[]{:S(2)}) copy-start(bf16[1,8,24,768]{3,2,1,0:T(8,128)(2,1)} %ag_hbm.3) | copy-start | bytes 884740
  7.8 1.0 %copy-start.6 = (bf16[1,2,96,768]{3,2,1,0:T(8,128)(2,1)S(1)}, bf16[1,2,96,768]{3,2,1,0:T(8,128)(2,1)}, u32[]{:S(2)}) copy-start(bf16[1,2,96,768]{3,2,1,0:T(8,128)(2,1)} %dg_hbm.3) | copy-start | bytes 884740
  8.7 43.2 %copy-start.7 = (f32[256,768]{1,0:T(8,128)S(1)}, f32[256,768]{1,0:T(8,128)}, u32[]{:S(2)}) copy-start(f32[256,768]{1,0:T(8,128)} %ew_hbm.1) | copy-start | bytes 2359300
  8.8 43.2 %copy-start.8 = (f32[256,768]{1,0:T(8,128)S(1)}, f32[256,768]{1,0:T(8,128)}, u32[]{:S(2)}) copy-start(f32[256,768]{1,0:T(8,128)} %em_hbm.1) | copy-start | bytes 2359300
  8.8 43.2 %copy-start.9 = (f32[8,24,768]{2,1,0:T(8,128)S(1)}, f32[8,24,768]{2,1,0:T(8,128)}, u32[]{:S(2)}) copy-start(f32[8,24,768]{2,1,0:T(8,128)} %aw_hbm.1) | copy-start | bytes 1769476
  8.8 43.2 %copy-start.10 = (f32[2,96,768]{2,1,0:T(8,128)S(1)}, f32[2,96,768]{2,1,0:T(8,128)}, u32[]{:S(2)}) copy-start(f32[2,96,768]{2,1,0:T(8,128)} %dw_hbm.1) | copy-start | bytes 1769476
  8.8 43.2 %copy-start.11 = (f32[8,24,768]{2,1,0:T(8,128)S(1)}, f32[8,24,768]{2,1,0:T(8,128)}, u32[]{:S(2)}) copy-start(f32[8,24,768]{2,1,0:T(8,128)} %am_hbm.1) | copy-start | bytes 1769476
  8.8 43.2 %copy-start.12 = (f32[2,96,768]{2,1,0:T(8,128)S(1)}, f32[2,96,768]{2,1,0:T(8,128)}, u32[]{:S(2)}) copy-start(f32[2,96,768]{2,1,0:T(8,128)} %dm_hbm.1) | copy-start | bytes 1769476
  8.8 43.2 %copy-start.13 = (f32[3,24]{1,0:T(4,128)S(1)}, f32[3,24]{1,0:T(4,128)}, u32[]{:S(2)}) copy-start(f32[3,24]{1,0:T(4,128)} %norm_scale.1) | copy-start | bytes 868
  8.8 43.2 %copy-start.14 = (f32[3,24]{1,0:T(4,128)S(1)}, f32[3,24]{1,0:T(4,128)}, u32[]{:S(2)}) copy-start(f32[3,24]{1,0:T(4,128)} %norm_momentum.1) | copy-start | bytes 868

commit v2 on v1

v2 whole, which is shorter than its diff:
```python
import jax
import jax.numpy as jnp
from jax import lax
from jax.experimental import pallas as pl
from jax.experimental.pallas import tpu as pltpu
from jax.sharding import PartitionSpec as P

MESH = pl.DeviceIdType.MESH
F32, BF16 = jnp.float32, jnp.bfloat16
D = 768
HALF = 384
RANK = 32
NMAT = 11
TILES = 3
LEFT = NMAT * RANK
ROWS = 640
AD_ROWS = 384
AD_LEFT = 10 * RANK
NT = (((1,), (1,)), ((), ()))
NN = (((1,), (0,)), ((), ()))
TN = (((0,), (0,)), ((), ()))


def hops(offset):
    return sum(min(d, 4 - d) for d in offset)


OTHERS = sorted(
    [(a, b, c) for a in range(4) for b in range(4) for c in range(4) if a or b or c],
    key=lambda offset: -hops(offset),
)


def split(x):
    hi = x.astype(BF16)
    return hi, (x - hi.astype(F32)).astype(BF16)


def dot(a, b, dims):
    return lax.dot_general(a, b, dims, preferred_element_type=F32)


def dot3(a, b, dims):
    (ah, al), (bh, bl) = a, b
    return dot(ah, bh, dims) + (dot(al, bh, dims) + dot(ah, bl, dims))


def exact(a, b, dims):
    return dot3(split(a), split(b), dims)


def row_mask(lefts, rows):
    m = lax.broadcasted_iota(jnp.int32, (lefts, rows), 0) // RANK
    r = lax.broadcasted_iota(jnp.int32, (lefts, rows), 1)
    low = jnp.where(m < 8, 24 * m, jnp.where(m < 10, 96 * m - 576, AD_ROWS))
    high = low + jnp.where(m < 8, 24, jnp.where(m < 10, 96, 256))
    return (r >= low) & (r < high)


def fold(x, blocks):
    total = x[:RANK]
    for m in range(1, blocks):
        total = total + x[m * RANK : (m + 1) * RANK]
    return total


def position():
    x, s = lax.axis_index("rep"), lax.axis_index("shard")
    return x, s // 2, s % 2


def device(x, plane, core):
    return (x, plane * 2 + core)


def exchange_kernel(
    ag_hbm, dg_hbm, eg_hbm, ae_hbm, de_hbm, ee_hbm, warm_hbm, norm_hbm, *rest,
):
    state_hbm = rest[:6]
    right_out, left_sum, norm_out, merged, warm = rest[6:11]
    state = rest[11:17]
    exchange_body(
        ag_hbm, dg_hbm, eg_hbm, ae_hbm, de_hbm, ee_hbm, warm_hbm, norm_hbm, state_hbm,
        right_out, left_sum, norm_out, merged, warm, state, *rest[17:],
    )


def exchange_body(
    ag_hbm, dg_hbm, eg_hbm, ae_hbm, de_hbm, ee_hbm, warm_hbm, norm_hbm, state_hbm,
    right, left_sum, norm_out, merged, warm, state,
    ag, dg, eg, ae, de, ee, norm, merged_hi, merged_lo,
    left_a, left_b, other, own, sibling, slots_a, slots_b, norm_slots,
    in_sem, left_send, left_recv, core_send, core_recv, rs_send, rs_recv,
    ag_send, ag_recv, tail_send, tail_recv, half_send, half_recv, norm_send, norm_recv,
):
    x, plane, core = position()
    chip = x * 16 + plane
    idle = chip % 21 == 0
    which = chip - 1 - chip // 21

    def block(q):
        return q % TILES, pl.ds(pl.multiple_of(16 * (q // TILES), 16), 16)

    def tail(r):
        return pl.ds(pl.multiple_of(AD_LEFT + 8 * r, 8), 8)

    xs = [x] + [(x + d) % 4 for d in range(1, 4)]
    zs = [plane // 4] + [(plane // 4 + d) % 4 for d in range(1, 4)]
    ys = [plane % 4] + [(plane % 4 + d) % 4 for d in range(1, 4)]

    barrier = pltpu.get_barrier_semaphore()
    pl.semaphore_signal(barrier, inc=1, device_id=device(x, plane, 1 - core), device_id_type=MESH)
    for d in range(1, 4):
        pl.semaphore_signal(barrier, inc=1, device_id=device((x + d) % 4, plane, core), device_id_type=MESH)

    def greet(i, carry):
        pl.semaphore_signal(barrier, inc=1, device_id=device(x, (plane + i) % 16, core), device_id_type=MESH)
        return carry

    lax.fori_loop(1, 16, greet, 0)

    loads = [
        pltpu.make_async_copy(a, b, in_sem.at[i])
        for i, (a, b) in enumerate(
            [(warm_hbm, warm), (ag_hbm, ag), (ae_hbm, ae), (dg_hbm, dg), (de_hbm, de), (eg_hbm, eg), (ee_hbm, ee), (norm_hbm, norm),
             *zip(state_hbm, state)]
        )
    ]
    for copy in loads[:8]:
        copy.start()

    def put(row, rows, value):
        merged[row : row + rows, :] = value
        hi, lo = split(value)
        for h in range(2):
            merged_hi[h, row : row + rows, :] = hi[:, h * HALF : (h + 1) * HALF]
            merged_lo[h, row : row + rows, :] = lo[:, h * HALF : (h + 1) * HALF]

    loads[0].wait()
    loads[1].wait()
    loads[2].wait()
    for m in range(0, 8, 2):
        put(24 * m, 48, jnp.concatenate(
            [ag[0, m].astype(F32) + ae[0, m], ag[0, m + 1].astype(F32) + ae[0, m + 1]], 0))
    loads[3].wait()
    loads[4].wait()
    for m in range(2):
        put(192 + 96 * m, 96, dg[0, m].astype(F32) + de[0, m])

    def project(first, last, row, rows, mask):
        w = split(warm[first:last].reshape((last - first) * RANK, D))
        total = None
        for h in range(2):
            part = dot3(
                [p[:, h * HALF : (h + 1) * HALF] for p in w],
                (merged_hi[h, row : row + rows, :], merged_lo[h, row : row + rows, :]),
                NT,
            )
            total = part if total is None else total + part
        if mask is not None:
            total = fold(jnp.where(mask, total, 0.0), last - first)
        return total

    mask = row_mask(AD_LEFT, AD_ROWS)
    left_a[x] = project(0, 10, 0, AD_ROWS, mask)

    pl.semaphore_wait(barrier, 19)

    def share(buf, i):
        return [
            pltpu.make_async_remote_copy(
                src_ref=buf.at[x], dst_ref=buf.at[x], send_sem=left_send.at[i, d - 1], recv_sem=left_recv.at[i, d - 1],
                device_id=device((x + d) % 4, plane, core), device_id_type=MESH)
            for d in range(1, 4)
        ]

    share_a = share(left_a, 0)
    for copy in share_a:
        copy.start()
    loads[5].wait()
    loads[6].wait()
    for m in range(2):
        put(AD_ROWS + 128 * m, 128, eg[0, 128 * m : 128 * m + 128].astype(F32) + ee[0, 128 * m : 128 * m + 128])
    left_b[x] = project(10, 11, AD_ROWS, 256, None)
    share_b = share(left_b, 1)
    for copy in share_b:
        copy.start()
    for copy in loads[8:]:
        copy.start()
    loads[7].wait()
    norm_slots[x] = jnp.zeros((8, 128), F32)
    for k in range(3):
        norm_slots[x, k : k + 1, 0:24] = norm[k]
    share_n = [
        pltpu.make_async_remote_copy(
            src_ref=norm_slots.at[x], dst_ref=norm_slots.at[x], send_sem=norm_send.at[d - 1], recv_sem=norm_recv.at[d - 1],
            device_id=device((x + d) % 4, plane, core), device_id_type=MESH)
        for d in range(1, 4)
    ]
    for copy in share_n:
        copy.start()

    def contract(left, half, row, rows):
        return dot3(left, (merged_hi[half, row : row + rows, :], merged_lo[half, row : row + rows, :]), NN)

    def store(ref, row, rows, value):
        for t in range(TILES):
            ref[t, row : row + rows, :] = value[:, 128 * t : 128 * t + 128]

    def swap(i, row, rows):
        return pltpu.make_async_remote_copy(
            src_ref=other.at[:, row : row + rows], dst_ref=sibling.at[:, row : row + rows], send_sem=core_send.at[i],
            recv_sem=core_recv.at[i], device_id=device(x, plane, 1 - core), device_id_type=MESH)

    for copy in share_a:
        copy.wait_recv()
    pa = (left_a[0] + left_a[1] + left_a[2] + left_a[3]) * 0.25
    left_sum[:, 0:AD_ROWS] = pa
    spread = split(jnp.where(mask, jnp.concatenate([pa] * 10, 0), 0.0))
    store(other, 0, AD_LEFT, contract(spread, 1 - core, 0, AD_ROWS))
    swap_a = swap(0, 0, AD_LEFT)
    swap_a.start()
    store(own, 0, AD_LEFT, contract(spread, core, 0, AD_ROWS))

    for copy in share_b:
        copy.wait_recv()
    pb = (left_b[0] + left_b[1] + left_b[2] + left_b[3]) * 0.25
    left_sum[:, AD_ROWS:ROWS] = pb
    pb = split(pb)
    store(other, AD_LEFT, RANK, contract(pb, 1 - core, AD_ROWS, 256))
    swap_b = swap(1, AD_LEFT, RANK)
    swap_b.start()
    store(own, AD_LEFT, RANK, contract(pb, core, AD_ROWS, 256))

    swap_a.wait_recv()
    own[:, 0:AD_LEFT, :] = own[:, 0:AD_LEFT, :] + sibling[:, 0:AD_LEFT, :]
    for dx, dz, dy in OTHERS:
        to = xs[dx] * 16 + zs[dz] * 4 + ys[dy]

        @pl.when(to % 21 != 0)
        def _():
            tile, rows = block(to - 1 - to // 21)
            pltpu.make_async_remote_copy(
                src_ref=own.at[tile, rows], dst_ref=slots_a.at[chip], send_sem=rs_send, recv_sem=rs_recv,
                device_id=device(xs[dx], zs[dz] * 4 + ys[dy], core), device_id_type=MESH).start()

    swap_b.wait_recv()
    own[:, AD_LEFT:LEFT, :] = own[:, AD_LEFT:LEFT, :] + sibling[:, AD_LEFT:LEFT, :]

    def tail_copies(phase, steps, src, dst, target):
        return [
            pltpu.make_async_remote_copy(
                src_ref=src(steps[d]), dst_ref=dst, send_sem=tail_send.at[phase, d - 1], recv_sem=tail_recv.at[phase, d - 1],
                device_id=target(steps[d]), device_id_type=MESH)
            for d in range(1, 4)
        ]

    def start_all(copies):
        for copy in copies:
            copy.start()
        return copies

    def sum_tails(phase, copies):
        for copy in copies:
            copy.wait_recv()
        return (slots_b[phase, 0] + slots_b[phase, 1]) + (slots_b[phase, 2] + slots_b[phase, 3])

    def at_z(z):
        return device(x, z * 4 + ys[0], core)

    slots_b[0, zs[0]] = own[:, tail(zs[0]), :]
    tails_z = start_all(tail_copies(0, zs, lambda z: own.at[:, tail(z)], slots_b.at[0, zs[0]], at_z))
    slots_b[1, x] = sum_tails(0, tails_z)
    part_x = slots_b.at[1, x]
    tails_x = start_all(tail_copies(1, xs, lambda _: part_x, part_x, lambda to: device(to, plane, core)))
    slots_b[2, ys[0]] = sum_tails(1, tails_x)
    part_y = slots_b.at[2, ys[0]]
    tails_y = start_all(tail_copies(2, ys, lambda _: part_y, part_y, lambda y: device(x, zs[0] * 4 + y, core)))

    def spread_out(part):
        for dx, dz, dy in OTHERS:
            pltpu.make_async_remote_copy(
                src_ref=part, dst_ref=part, send_sem=ag_send, recv_sem=ag_recv.at[x],
                device_id=device(xs[dx], zs[dz] * 4 + ys[dy], core), device_id_type=MESH).start()

    def drain(part, sem):
        pltpu.make_async_copy(part, part, sem).wait()

    @pl.when(jnp.logical_not(idle))
    def _():
        tile, rows = block(which)
        slots_a[chip] = own[tile, rows, :]
        drain(slots_a.at[0:63], rs_recv)
        right[core, tile, rows, :] = lax.fori_loop(1, 64, lambda i, t: t + slots_a[i], slots_a[0]) * 0.25
        spread_out(right.at[core, tile, rows])

    right[core, :, tail(zs[0]), :] = sum_tails(2, tails_y) * 0.25
    part_z = right.at[core, :, tail(zs[0])]
    tails_end = start_all(tail_copies(3, zs, lambda _: part_z, part_z, at_z))

    forwards = []

    def forward(rows):
        part = right.at[core, :, rows]
        copy = pltpu.make_async_remote_copy(
            src_ref=part, dst_ref=part, send_sem=half_send.at[len(forwards)], recv_sem=half_recv.at[len(forwards)],
            device_id=device(x, plane, 1 - core), device_id_type=MESH)
        copy.start()
        forwards.append(copy)

    for d in (0, 1, 3, 2):
        from_x = xs[d]
        if d == 0:

            @pl.when(idle)
            def _():
                drain(slots_a.at[0:15], ag_recv.at[x])

            @pl.when(jnp.logical_not(idle))
            def _():
                drain(slots_a.at[0:14], ag_recv.at[x])
        else:
            drain(slots_a.at[0:15], ag_recv.at[from_x])
        forward(pl.ds(pl.multiple_of(80 * from_x, 16), 80))

    for copy in tails_end:
        copy.wait_recv()
    forward(pl.ds(AD_LEFT, RANK))
    for copy in share_n:
        copy.wait_recv()
    norm_out[...] = norm_slots[0] + norm_slots[1] + norm_slots[2] + norm_slots[3]
    for copy in forwards:
        copy.wait_recv()
    for copy in share_a + share_b + share_n + [swap_a, swap_b] + tails_z + tails_x + tails_y + tails_end + forwards:
        copy.wait_send()

    @pl.when(idle)
    def _():
        drain(slots_a.at[0:60], rs_send)

    @pl.when(jnp.logical_not(idle))
    def _():
        drain(slots_a.at[0:59], rs_send)
        drain(slots_a.at[0:63], ag_send)

    for copy in loads[8:]:
        copy.wait()

def invert(gram):
    lane = lax.broadcasted_iota(jnp.int32, (8, 128), 1)
    column = lane % RANK
    base = lane - column
    sub = lax.broadcasted_iota(jnp.int32, (8, 128), 0)
    a = [[gram[8 * g : 8 * g + 8, 128 * l : 128 * l + 128] for l in range(3)] for g in range(4)]
    for p in range(RANK):
        gp, sp = p // 8, p % 8
        for l in range(3):
            index = base + p
            pick = [jnp.take_along_axis(a[g][l], index, axis=1) for g in range(gp, 4)]
            pivot = pick[0][sp : sp + 1, :]
            row = jnp.where(column[:1] == p, 1.0, a[gp][l][sp : sp + 1, :]) / pivot
            for g in range(gp, 4):
                f = pick[g - gp]
                keep = jnp.where(column == p, 0.0, a[g][l])
                new = keep - f * row
                a[g][l] = jnp.where(sub > sp, new, a[g][l]) if g == gp else new
    out = []
    for g in range(4):
        parts = []
        for l in range(3):
            i = sub + 8 * g
            pivot = jnp.take_along_axis(a[g][l], base + i, axis=1)
            value = jnp.where(column < i, a[g][l], jnp.where(column == i, 1.0, 0.0))
            parts.append(value / jnp.sqrt(pivot))
        out.append(jnp.concatenate(parts, 1))
    return jnp.concatenate(out, 0)


def finish_kernel(
    merged, aw, dw, ew, am, dm, em, warm, right, left, norm_total, norm_scale, norm_momentum,
    au_hbm, du_hbm, eu_hbm, ac_hbm, dc_hbm, ec_hbm, ar_hbm, dr_hbm, er_hbm, av_hbm, dv_hbm, ev_hbm,
    next_hbm, norm_updated, norm_velocity,
    au, du, eu, ac, dc, ec, ar, dr, er, av, dv, ev, start, wide, out_sem,
):
    velocity = 0.9 * norm_momentum[...] + norm_total[0:3, 0:24] / 4
    norm_velocity[...] = velocity
    norm_updated[...] = norm_scale[...] - 0.05 * velocity

    wide[LEFT:, :] = jnp.zeros((32, D), F32)
    wide[0:LEFT, :] = warm[...].reshape(LEFT, D)
    factor = jnp.concatenate([right[h, t] for h in range(2) for t in range(TILES)], 1)
    gram = exact(factor, wide[...], NT)
    mi = lax.broadcasted_iota(jnp.int32, (LEFT, HALF), 0) // RANK
    mj = lax.broadcasted_iota(jnp.int32, (LEFT, HALF), 1) // RANK
    same = mi == mj
    gram = fold(jnp.where(same, gram, 0.0), NMAT)
    i = lax.broadcasted_iota(jnp.int32, (RANK, HALF), 0)
    j = lax.broadcasted_iota(jnp.int32, (RANK, HALF), 1)
    gram = jnp.where(j < LEFT, gram, jnp.where(i == j - LEFT, 1.0, 0.0))
    inverse = invert(gram)
    inverse = jnp.where(same, jnp.concatenate([inverse] * NMAT, 0), 0.0)[:, 0:LEFT]
    start[...] = exact(inverse, factor, NN)
    copies = []

    def send(src, dst):
        copy = pltpu.make_async_copy(src, dst, out_sem.at[len(copies)])
        copy.start()
        copies.append(copy)

    send(start, next_hbm)
    spread = jnp.where(row_mask(LEFT, ROWS), jnp.concatenate([left[...]] * NMAT, 0), 0.0)
    ortho = exact(inverse, spread, NN)
    oh, ol = split(ortho)
    oh, ol = oh.T, ol.T
    sh, sl = split(start[...])

    def approx(row, rows):
        part = slice(row, row + rows)
        return dot3((oh[part], ol[part]), (sh, sl), NN)

    def write(value, row, rows, w, m, u, c, r, v):
        r[...] = merged[row : row + rows, :] - value
        velocity = 0.9 * m[...] + value
        updated = w[...] - 0.05 * velocity
        v[...] = velocity
        u[...] = updated
        c[...] = updated.astype(BF16)

    value = approx(0, 192)
    for m in range(8):
        write(value[24 * m : 24 * m + 24], 24 * m, 24, aw.at[m], am.at[m],
              au.at[m], ac.at[m], ar.at[0, m], av.at[m])
    for a, b in ((au, au_hbm), (ac, ac_hbm), (ar, ar_hbm), (av, av_hbm)):
        send(a, b)
    for m in range(2):
        write(approx(192 + 96 * m, 96), 192 + 96 * m, 96, dw.at[m], dm.at[m],
              du.at[m], dc.at[m], dr.at[0, m], dv.at[m])
    for a, b in ((du, du_hbm), (dc, dc_hbm), (dr, dr_hbm), (dv, dv_hbm)):
        send(a, b)
    for m in range(2):
        part = pl.ds(128 * m, 128)
        write(approx(AD_ROWS + 128 * m, 128), AD_ROWS + 128 * m, 128, ew.at[part], em.at[part],
              eu.at[part], ec.at[part], er.at[0, part], ev.at[part])
        for a, b in ((eu, eu_hbm), (ec, ec_hbm), (ev, ev_hbm)):
            send(a.at[part], b.at[part])
        send(er.at[0, part], er_hbm.at[0, part])
    for copy in copies:
        copy.wait()


ANY = pl.BlockSpec(memory_space=pl.ANY)
VMEM = pl.BlockSpec(memory_space=pltpu.VMEM)
DMA = pltpu.SemaphoreType.DMA


def body(
    attention_grad, dense_grad, embedding_grad, attention_error, dense_error, embedding_error,
    attention_weight, dense_weight, embedding_weight, attention_momentum, dense_momentum, embedding_momentum,
    warm_start, norm_scale, norm_momentum, norm_grad,
):
    def pin(*arrays):
        return [pltpu.with_memory_space_constraint(a, pltpu.HBM) for a in arrays]

    grads = pin(attention_grad, dense_grad, embedding_grad)
    errors = pin(attention_error, dense_error, embedding_error)
    weights = pin(attention_weight, dense_weight, embedding_weight)
    momenta = pin(attention_momentum, dense_momentum, embedding_momentum)
    state = weights + momenta

    def like(arrays, dtype=None):
        return [pltpu.VMEM(a.shape, dtype or a.dtype) for a in arrays]

    def shape(a, dtype=None):
        return jax.ShapeDtypeStruct(a.shape, dtype or a.dtype)

    right, left, norm_total, merged, warm, *state = pl.pallas_call(
        exchange_kernel,
        name="exchange",
        out_shape=(
            jax.ShapeDtypeStruct((2, TILES, LEFT, 128), F32),
            jax.ShapeDtypeStruct((RANK, ROWS), F32),
            jax.ShapeDtypeStruct((8, 128), F32),
            jax.ShapeDtypeStruct((ROWS, D), F32),
            shape(warm_start),
            *[shape(a) for a in state],
        ),
        in_specs=[ANY] * 14,
        out_specs=(VMEM,) * 11,
        scratch_shapes=like(grads) + like(errors) + [
            pltpu.VMEM((3, 1, 24), F32),
            pltpu.VMEM((2, ROWS, HALF), BF16),
            pltpu.VMEM((2, ROWS, HALF), BF16),
            pltpu.VMEM((4, RANK, AD_ROWS), F32),
            pltpu.VMEM((4, RANK, 256), F32),
            pltpu.VMEM((TILES, LEFT, 128), F32),
            pltpu.VMEM((TILES, LEFT, 128), F32),
            pltpu.VMEM((TILES, LEFT, 128), F32),
            pltpu.VMEM((64, 16, 128), F32),
            pltpu.VMEM((3, 4, TILES, 8, 128), F32),
            pltpu.VMEM((4, 8, 128), F32),
            DMA((14,)), DMA((2, 3)), DMA((2, 3)), DMA((2,)), DMA((2,)), DMA, DMA,
            DMA, DMA((4,)), DMA((4, 3)), DMA((4, 3)), DMA((5,)), DMA((5,)), DMA((3,)), DMA((3,)),
        ],
        compiler_params=pltpu.CompilerParams(collective_id=0, has_side_effects=True, vmem_limit_bytes=20 << 20),
    )(*grads, *errors, *pin(warm_start, jnp.transpose(norm_grad, (1, 0, 2))), *state)

    shapes = [
        *[jax.ShapeDtypeStruct(a.shape, F32) for a in weights],
        *[jax.ShapeDtypeStruct(a.shape, BF16) for a in weights],
        *[jax.ShapeDtypeStruct(a.shape, F32) for a in errors],
        *[jax.ShapeDtypeStruct(a.shape, F32) for a in weights],
        jax.ShapeDtypeStruct((LEFT, D), F32),
        jax.ShapeDtypeStruct(norm_scale.shape, F32),
        jax.ShapeDtypeStruct(norm_scale.shape, F32),
    ]
    outs = pl.pallas_call(
        finish_kernel,
        name="finish",
        out_shape=tuple(shapes),
        in_specs=[VMEM] * 13,
        out_specs=tuple([ANY] * 13 + [VMEM] * 2),
        scratch_shapes=like(weights) + like(weights, BF16) + like(errors) + like(weights) + [
            pltpu.VMEM((LEFT, D), F32), pltpu.VMEM((HALF, D), F32), DMA((17,)),
        ],
        compiler_params=pltpu.CompilerParams(vmem_limit_bytes=24 << 20),
    )(merged, *state, warm, right, left, norm_total, norm_scale, norm_momentum)
    outs = list(outs)
    outs[12] = outs[12].reshape(NMAT, RANK, D)
    return tuple(outs)


def solution(mesh):
    matrices = (P(None, "shard", None), P(None, "shard", None), P("shard", None))
    replicas = (P("rep", None, "shard", None), P("rep", None, "shard", None), P("rep", "shard", None))
    norm = P(None, "shard")
    return jax.shard_map(
        body,
        mesh=mesh,
        in_specs=replicas + replicas + matrices + matrices + (P(), norm, norm, P("rep", None, "shard")),
        out_specs=matrices + matrices + replicas + matrices + (P(), norm, norm),
        check_vma=False,
    )
```

time: 69.4 us -> 52.8 us (0.76)
  local copies, waits for them, and re-layouts: 8.14 us -> 0.01 us
  Pallas kernels: 59.9 us -> 52 us
    unnamed x31 -> x4, local copies, waits for them, and re-layouts: 8.14 us -> 0.01 us
    pallas_call x1, Pallas kernels: 16.8 us -> 11.1 us  [body(): pl.pallas_call(finish_kernel, name='finish', out_shape=tuple(shapes), in_...]
    pallas_call x1, Pallas kernels: 43.1 us -> 40.9 us  [body(): pl.pallas_call(exchange_kernel, name='exchange', out_shape=(jax.ShapeDtyp...]
where the time goes in v2:
time: 52.8 us; the launch traced here: 52.7 us
  Pallas kernels  52 us (98%)
  between operations  0.69 us (1%)
    pallas_call x1, Pallas kernels, body(): pl.pallas_call(exchange_kernel, name='exchange', out_shape=(jax.ShapeDtyp...  40.9 us
    pallas_call x1, Pallas kernels, body(): pl.pallas_call(finish_kernel, name='finish', out_shape=tuple(shapes), in_...  11.1 us

profile of v2, /device:TPU:1, one launch (start us, length us, event | category | flops | bytes accessed | tf_op | source)
XLA Modules:
  0.0 52.7 jit_solution(9454060068380943692)
XLA Ops:
  0.7 0.0 copy-start
  0.7 0.0 copy-start.1
  0.7 40.9 %exchange.1 = (f32[2,3,352,128]{3,2,1,0:T(8,128)S(1)}, f32[32,640]{1,0:T(8,128)S(1)}, f32[8,128]{1,0:T(8,128)S(1)}, f32[640,768]{1,0:T(8,128)S(1)}, f32[11,32,76...) custom-call(bf16[1,8,24,768]{3,2,1,0:T(8,128)(2,1)} %ag_hbm.1, ...), custom_call_target="tpu_custom_call" | custom-call | tf_op jit(solution)/shard_map/exchange/pallas_call | solution.py:476
  41.5 0.0 copy-done
  41.5 0.0 copy-done.1
  41.6 11.1 %finish.1 = (f32[8,24,768]{2,1,0:T(8,128)}, f32[2,96,768]{2,1,0:T(8,128)}, f32[256,768]{1,0:T(8,128)}, bf16[8,24,768]{2,1,0:T(8,128)(2,1)}, bf16[2,96,768]{2,1,0...) custom-call(f32[640,768]{1,0:T(8,128)S(1)} %get-tuple-element.41.mer, ...), custom_call_target="tpu_custom_call" | custom-call | tf_op jit(solution)/shard_map/finish/pallas_call | solution.py:516
Async XLA Ops:
  0.7 40.9 %copy-start = (f32[3,24]{1,0:T(4,128)S(1)}, f32[3,24]{1,0:T(4,128)}, u32[]{:S(2)}) copy-start(f32[3,24]{1,0:T(4,128)} %norm_scale.1) | copy-start | bytes 868
  0.7 40.9 %copy-start.1 = (f32[3,24]{1,0:T(4,128)S(1)}, f32[3,24]{1,0:T(4,128)}, u32[]{:S(2)}) copy-start(f32[3,24]{1,0:T(4,128)} %norm_momentum.1) | copy-start | bytes 868

commit v3 on v2

--- a/solution.py
+++ b/solution.py
@@ -234,15 +234,16 @@
 
     swap_a.wait_recv()
     own[:, 0:AD_LEFT, :] = own[:, 0:AD_LEFT, :] + sibling[:, 0:AD_LEFT, :]
-    for dx, dz, dy in OTHERS:
-        to = xs[dx] * 16 + zs[dz] * 4 + ys[dy]
-
-        @pl.when(to % 21 != 0)
-        def _():
-            tile, rows = block(to - 1 - to // 21)
-            pltpu.make_async_remote_copy(
-                src_ref=own.at[tile, rows], dst_ref=slots_a.at[chip], send_sem=rs_send, recv_sem=rs_recv,
-                device_id=device(xs[dx], zs[dz] * 4 + ys[dy], core), device_id_type=MESH).start()
+    def scatter(others):
+        for dx, dz, dy in others:
+            to = xs[dx] * 16 + zs[dz] * 4 + ys[dy]
+
+            @pl.when(to % 21 != 0)
+            def _():
+                tile, rows = block(to - 1 - to // 21)
+                pltpu.make_async_remote_copy(
+                    src_ref=own.at[tile, rows], dst_ref=slots_a.at[chip], send_sem=rs_send, recv_sem=rs_recv,
+                    device_id=device(xs[dx], zs[dz] * 4 + ys[dy], core), device_id_type=MESH).start()
 
     swap_b.wait_recv()
     own[:, AD_LEFT:LEFT, :] = own[:, AD_LEFT:LEFT, :] + sibling[:, AD_LEFT:LEFT, :]
@@ -270,6 +271,7 @@
 
     slots_b[0, zs[0]] = own[:, tail(zs[0]), :]
     tails_z = start_all(tail_copies(0, zs, lambda z: own.at[:, tail(z)], slots_b.at[0, zs[0]], at_z))
+    scatter(OTHERS)
     slots_b[1, x] = sum_tails(0, tails_z)
     part_x = slots_b.at[1, x]
     tails_x = start_all(tail_copies(1, xs, lambda _: part_x, part_x, lambda to: device(to, plane, core)))
@@ -291,7 +293,7 @@
         tile, rows = block(which)
         slots_a[chip] = own[tile, rows, :]
         drain(slots_a.at[0:63], rs_recv)
-        right[core, tile, rows, :] = lax.fori_loop(1, 64, lambda i, t: t + slots_a[i], slots_a[0]) * 0.25
+        right[core, tile, rows, :] = jnp.sum(slots_a[...], axis=0) * 0.25
         spread_out(right.at[core, tile, rows])
 
     right[core, :, tail(zs[0]), :] = sum_tails(2, tails_y) * 0.25
@@ -352,12 +354,17 @@
     base = lane - column
     sub = lax.broadcasted_iota(jnp.int32, (8, 128), 0)
     a = [[gram[8 * g : 8 * g + 8, 128 * l : 128 * l + 128] for l in range(3)] for g in range(4)]
+    picks = [[jnp.take_along_axis(a[g][l], base, axis=1) for g in range(4)] for l in range(3)]
     for p in range(RANK):
         gp, sp = p // 8, p % 8
         for l in range(3):
-            index = base + p
-            pick = [jnp.take_along_axis(a[g][l], index, axis=1) for g in range(gp, 4)]
+            pick = picks[l]
             pivot = pick[0][sp : sp + 1, :]
+            if p + 1 < RANK:
+                ahead = [jnp.take_along_axis(a[g][l], base + p + 1, axis=1) for g in range(gp, 4)]
+                ratio = ahead[0][sp : sp + 1, :] / pivot
+                ahead = [c - f * ratio for c, f in zip(ahead, pick)]
+                picks[l] = ahead[(p + 1) // 8 - gp :]
             row = jnp.where(column[:1] == p, 1.0, a[gp][l][sp : sp + 1, :]) / pivot
             for g in range(gp, 4):
                 f = pick[g - gp]

time: 52.8 us -> 48.6 us (0.920)
  Pallas kernels: 52 us -> 47.8 us
    pallas_call x1, Pallas kernels: 40.9 us -> 37.8 us  [body(): pl.pallas_call(exchange_kernel, name='exchange', out_shape=(jax.ShapeDtyp...]
    pallas_call x1, Pallas kernels: 11.1 us -> 10 us  [body(): pl.pallas_call(finish_kernel, name='finish', out_shape=tuple(shapes), in_...]
where the time goes in v3:
time: 48.6 us; the launch traced here: 48.5 us
  Pallas kernels  47.8 us (98%)
  between operations  0.69 us (1%)
    pallas_call x1, Pallas kernels, body(): pl.pallas_call(exchange_kernel, name='exchange', out_shape=(jax.ShapeDtyp...  37.8 us
    pallas_call x1, Pallas kernels, body(): pl.pallas_call(finish_kernel, name='finish', out_shape=tuple(shapes), in_...  10 us

profile of v3, /device:TPU:1, one launch (start us, length us, event | category | flops | bytes accessed | tf_op | source)
XLA Modules:
  0.0 48.5 jit_solution(2120117929112763127)
XLA Ops:
  0.7 0.0 copy-start
  0.7 0.0 copy-start.1
  0.7 37.8 %exchange.1 = (f32[2,3,352,128]{3,2,1,0:T(8,128)S(1)}, f32[32,640]{1,0:T(8,128)S(1)}, f32[8,128]{1,0:T(8,128)S(1)}, f32[640,768]{1,0:T(8,128)S(1)}, f32[11,32,76...) custom-call(bf16[1,8,24,768]{3,2,1,0:T(8,128)(2,1)} %ag_hbm.1, ...), custom_call_target="tpu_custom_call" | custom-call | tf_op jit(solution)/shard_map/exchange/pallas_call | solution.py:483
  38.5 0.0 copy-done
  38.5 0.0 copy-done.1
  38.5 10.0 %finish.1 = (f32[8,24,768]{2,1,0:T(8,128)}, f32[2,96,768]{2,1,0:T(8,128)}, f32[256,768]{1,0:T(8,128)}, bf16[8,24,768]{2,1,0:T(8,128)(2,1)}, bf16[2,96,768]{2,1,0...) custom-call(f32[640,768]{1,0:T(8,128)S(1)} %get-tuple-element.41.mer, ...), custom_call_target="tpu_custom_call" | custom-call | tf_op jit(solution)/shard_map/finish/pallas_call | solution.py:523
Async XLA Ops:
  0.7 37.9 %copy-start = (f32[3,24]{1,0:T(4,128)S(1)}, f32[3,24]{1,0:T(4,128)}, u32[]{:S(2)}) copy-start(f32[3,24]{1,0:T(4,128)} %norm_scale.1) | copy-start | bytes 868
  0.7 37.9 %copy-start.1 = (f32[3,24]{1,0:T(4,128)S(1)}, f32[3,24]{1,0:T(4,128)}, u32[]{:S(2)}) copy-start(f32[3,24]{1,0:T(4,128)} %norm_momentum.1) | copy-start | bytes 868

commit v4 on v3

--- a/solution.py
+++ b/solution.py
@@ -433,12 +433,15 @@
         u[...] = updated
         c[...] = updated.astype(BF16)
 
-    value = approx(0, 192)
-    for m in range(8):
-        write(value[24 * m : 24 * m + 24], 24 * m, 24, aw.at[m], am.at[m],
-              au.at[m], ac.at[m], ar.at[0, m], av.at[m])
-    for a, b in ((au, au_hbm), (ac, ac_hbm), (ar, ar_hbm), (av, av_hbm)):
-        send(a, b)
+    for m in range(0, 8, 4):
+        value = approx(24 * m, 96)
+        for k in range(4):
+            write(value[24 * k : 24 * k + 24], 24 * (m + k), 24, aw.at[m + k], am.at[m + k],
+                  au.at[m + k], ac.at[m + k], ar.at[0, m + k], av.at[m + k])
+        part = pl.ds(m, 4)
+        for a, b in ((au, au_hbm), (ac, ac_hbm), (av, av_hbm)):
+            send(a.at[part], b.at[part])
+        send(ar.at[0, part], ar_hbm.at[0, part])
     for m in range(2):
         write(approx(192 + 96 * m, 96), 192 + 96 * m, 96, dw.at[m], dm.at[m],
               du.at[m], dc.at[m], dr.at[0, m], dv.at[m])
@@ -527,7 +530,7 @@
         in_specs=[VMEM] * 13,
         out_specs=tuple([ANY] * 13 + [VMEM] * 2),
         scratch_shapes=like(weights) + like(weights, BF16) + like(errors) + like(weights) + [
-            pltpu.VMEM((LEFT, D), F32), pltpu.VMEM((HALF, D), F32), DMA((17,)),
+            pltpu.VMEM((LEFT, D), F32), pltpu.VMEM((HALF, D), F32), DMA((21,)),
         ],
         compiler_params=pltpu.CompilerParams(vmem_limit_bytes=24 << 20),
     )(merged, *state, warm, right, left, norm_total, norm_scale, norm_momentum)

time: 48.6 us -> 48.1 us (0.990)
  Pallas kernels: 47.8 us -> 47.3 us
    pallas_call x1, Pallas kernels: 10 us -> 9.44 us  [body(): pl.pallas_call(finish_kernel, name='finish', out_shape=tuple(shapes), in_...]
where the time goes in v4:
time: 48.1 us; the launch traced here: 48 us
  Pallas kernels  47.3 us (98%)
  between operations  0.69 us (1%)
    pallas_call x1, Pallas kernels, body(): pl.pallas_call(exchange_kernel, name='exchange', out_shape=(jax.ShapeDtyp...  37.8 us
    pallas_call x1, Pallas kernels, body(): pl.pallas_call(finish_kernel, name='finish', out_shape=tuple(shapes), in_...  9.44 us

profile of v4, /device:TPU:1, one launch (start us, length us, event | category | flops | bytes accessed | tf_op | source)
XLA Modules:
  0.0 48.0 jit_solution(15528813032773388199)
XLA Ops:
  0.7 0.0 copy-start
  0.7 0.0 copy-start.1
  0.7 37.8 %exchange.1 = (f32[2,3,352,128]{3,2,1,0:T(8,128)S(1)}, f32[32,640]{1,0:T(8,128)S(1)}, f32[8,128]{1,0:T(8,128)S(1)}, f32[640,768]{1,0:T(8,128)S(1)}, f32[11,32,76...) custom-call(bf16[1,8,24,768]{3,2,1,0:T(8,128)(2,1)} %ag_hbm.1, ...), custom_call_target="tpu_custom_call" | custom-call | tf_op jit(solution)/shard_map/exchange/pallas_call | solution.py:486
  38.5 0.0 copy-done
  38.5 0.0 copy-done.1
  38.5 9.4 %finish.1 = (f32[8,24,768]{2,1,0:T(8,128)}, f32[2,96,768]{2,1,0:T(8,128)}, f32[256,768]{1,0:T(8,128)}, bf16[8,24,768]{2,1,0:T(8,128)(2,1)}, bf16[2,96,768]{2,1,0...) custom-call(f32[640,768]{1,0:T(8,128)S(1)} %get-tuple-element.41.mer, ...), custom_call_target="tpu_custom_call" | custom-call | tf_op jit(solution)/shard_map/finish/pallas_call | solution.py:526
Async XLA Ops:
  0.7 37.9 %copy-start = (f32[3,24]{1,0:T(4,128)S(1)}, f32[3,24]{1,0:T(4,128)}, u32[]{:S(2)}) copy-start(f32[3,24]{1,0:T(4,128)} %norm_scale.1) | copy-start | bytes 868
  0.7 37.9 %copy-start.1 = (f32[3,24]{1,0:T(4,128)S(1)}, f32[3,24]{1,0:T(4,128)}, u32[]{:S(2)}) copy-start(f32[3,24]{1,0:T(4,128)} %norm_momentum.1) | copy-start | bytes 868
